TPU v7x, 32 devices: a whole 2x2x4 slice. The times are simulated.
32 devices in a mesh: shard: 2 (over x), ctx: 4 (over z), tp: 4 (over y, core).
Axes of the slice: x: 2, y: 2, z: 4, core: 2. Of those that a mesh axis runs over, the one named last changes fastest.
Arguments:
- frames: bfloat16 [2, 2, 2048, 1280], P(None, 'shard', 'ctx'), may hold values from -6 to 6
- lengths: int32 [2, 2], P(None, 'shard'), may hold values from 0 to 2048, as said below
- first_gain: bfloat16 [1280], replicated, may hold values from 0.25 to 1.75
- first_bias: bfloat16 [1280], replicated, may hold values from -3 to 3
- query_weight: bfloat16 [1280, 1280], P('shard', 'tp'), may hold values from -0.15625 to 0.15625
- query_bias: bfloat16 [1280], P('tp'), may hold values from -3 to 3
- key_weight: bfloat16 [1280, 1280], P('shard', 'tp'), may hold values from -0.15625 to 0.15625
- value_weight: bfloat16 [1280, 1280], P('shard', 'tp'), may hold values from -0.15625 to 0.15625
- value_bias: bfloat16 [1280], P('tp'), may hold values from -0.088378906 to 0.088378906
- output_weight: bfloat16 [1280, 1280], P('shard', 'tp'), may hold values from -4 to 4
- output_bias: bfloat16 [1280], replicated, may hold values from -3 to 3
- second_gain: bfloat16 [1280], replicated, may hold values from 0.25 to 1.75
- second_bias: bfloat16 [1280], replicated, may hold values from -3 to 3
- inner_weight: bfloat16 [1280, 5120], P('shard', 'tp'), may hold values from -0.15625 to 0.15625
- inner_bias: bfloat16 [5120], P('tp'), may hold values from -3 to 3
- outer_weight: bfloat16 [1280, 5120], P('shard', 'tp'), may hold values from -0.15625 to 0.15625
- outer_bias: bfloat16 [1280], replicated, may hold values from -3 to 3
- cotangent: bfloat16 [2, 2, 2048, 1280], P(None, 'shard', 'ctx'), may hold values from -6 to 6
Outputs:
- result: bfloat16 [2, 2, 2048, 1280], P(None, 'shard', 'ctx')
- frames_grad: bfloat16 [2, 2, 2048, 1280], P(None, 'shard', 'ctx')
- first_gain_grad: float32 [1280], replicated
- first_bias_grad: float32 [1280], replicated
- query_weight_grad: float32 [1280, 1280], P('shard', 'tp')
- query_bias_grad: float32 [1280], P('tp')
- key_weight_grad: float32 [1280, 1280], P('shard', 'tp')
- value_weight_grad: float32 [1280, 1280], P('shard', 'tp')
- value_bias_grad: float32 [1280], P('tp')
- output_weight_grad: float32 [1280, 1280], P('shard', 'tp')
- output_bias_grad: float32 [1280], replicated
- second_gain_grad: float32 [1280], replicated
- second_bias_grad: float32 [1280], replicated
- inner_weight_grad: float32 [1280, 5120], P('shard', 'tp')
- inner_bias_grad: float32 [5120], P('tp')
- outer_weight_grad: float32 [1280, 5120], P('shard', 'tp')
- outer_bias_grad: float32 [1280], replicated
Inputs may be any that keep to these rules, and one draw needn't show every extreme that they name: Slot lengths count a clip's first frames; 0 marks an empty slot; in every draw some slot is empty and some slot is full.
All inputs are finite; a program needn't handle non-finite values.
Results may differ from a plain program's by a relative error of at most 0.025.
Values may be sent and summed in bfloat16 or wider, within the bound.
No kernel may reach another device: no remote copies, remote signals or barrier semaphores. Data moves between devices by JAX's collectives and lax.ppermute only.
A program may use at most 192 MiB of HBM per device.

v0:
```python
import math
import jax
import jax.numpy as jnp
from jax import lax
from jax.sharding import PartitionSpec as P

HD = 80
epsilon = 1e-05


def layer_norm(values, scale_gain, shift_bias):
    center = values - jnp.mean(values, -1, keepdims=True)
    spread = jnp.mean(center * center, -1, keepdims=True)
    return center * lax.rsqrt(spread + epsilon) * scale_gain + shift_bias


def per_device(
    frames,
    lengths,
    first_gain,
    first_bias,
    query_weight,
    query_bias,
    key_weight,
    value_weight,
    value_bias,
    output_weight,
    output_bias,
    second_gain,
    second_bias,
    inner_weight,
    inner_bias,
    outer_weight,
    outer_bias,
    cotangent,
):
    float_kind = jnp.float32
    half_kind = jnp.bfloat16
    batch_count = frames.shape[0]
    frame_rows = frames.shape[2]
    group_width = query_weight.shape[1]
    head_count = group_width // HD
    scaling = 1.0 / math.sqrt(HD)
    slot_frames = frame_rows * lax.axis_size("ctx")
    key_block = min(512, slot_frames)
    positions = lax.axis_index("ctx") * frame_rows + jnp.arange(frame_rows, dtype=jnp.int32)
    gain_one = first_gain.astype(float_kind)
    bias_one = first_bias.astype(float_kind)
    gain_two = second_gain.astype(float_kind)
    bias_two = second_bias.astype(float_kind)
    query_shift = query_bias.astype(float_kind)
    value_shift = value_bias.astype(float_kind)
    output_shift = output_bias.astype(float_kind)
    inner_shift = inner_bias.astype(float_kind)
    outer_shift = outer_bias.astype(float_kind)
    shards = (query_weight, key_weight, value_weight, output_weight, inner_weight, outer_weight)
    contract_last = (((1,), (1,)), ((), ()))
    contract_rows = (((0,), (0,)), ((), ()))
    results = []
    frame_grads = []
    small_totals = None
    weight_totals = None
    for batch_index in range(batch_count):
        gathered = (
            lax.all_gather(shards[0], "shard", axis=0, tiled=True),
            lax.all_gather(shards[1], "shard", axis=0, tiled=True),
            lax.all_gather(shards[2], "shard", axis=0, tiled=True),
            lax.all_gather(shards[3], "shard", axis=0, tiled=True),
            lax.all_gather(shards[4], "shard", axis=0, tiled=True),
            lax.all_gather(shards[5], "shard", axis=0, tiled=True),
        )
        full_query, full_key, full_value, full_output, full_inner, full_outer = gathered
        clip_frames = frames[batch_index, 0].astype(float_kind)
        length = lengths[batch_index, 0]
        frame_valid = positions < length
        has_frames = length > 0
        normed, first_back = jax.vjp(layer_norm, clip_frames, gain_one, bias_one)
        normed_low = normed.astype(half_kind)
        queries = (
            jnp.dot(normed_low, full_query, preferred_element_type=float_kind) + query_shift
        ).astype(half_kind)
        key_rows = jnp.dot(normed_low, full_key, preferred_element_type=float_kind).astype(
            half_kind
        )
        value_rows = (
            jnp.dot(normed_low, full_value, preferred_element_type=float_kind) + value_shift
        ).astype(half_kind)
        query_heads = queries.reshape(frame_rows, head_count, HD)
        start = jnp.int32(0)
        key_piece = lax.all_gather(key_rows, "ctx", axis=0, tiled=True)
        value_piece = lax.all_gather(value_rows, "ctx", axis=0, tiled=True)
        unnormal = jnp.zeros((frame_rows, head_count, HD), float_kind)
        weight_total = jnp.zeros((frame_rows, head_count), float_kind)
        piece_rows = key_piece.shape[0]
        for begin in range(0, piece_rows, key_block):
            count = min(key_block, piece_rows - begin)
            key_part = key_piece[begin : begin + count].reshape(count, head_count, HD)
            value_part = value_piece[begin : begin + count].reshape(count, head_count, HD)
            scores = (
                jnp.einsum("qhd,khd->hqk", query_heads, key_part, preferred_element_type=float_kind)
                * scaling
            )
            key_valid = start + begin + jnp.arange(count, dtype=jnp.int32) < length
            expo = jnp.where(key_valid[None, None, :], jnp.exp(scores), 0.0)
            weight_total = weight_total + jnp.sum(expo, -1).T
            unnormal = unnormal + jnp.einsum(
                "hqk,khd->qhd",
                expo.astype(half_kind),
                value_part,
                preferred_element_type=float_kind,
            )
        unnormal, weight_total = (unnormal, weight_total)
        denominator = jnp.where(has_frames, weight_total, 1.0)
        attended = unnormal / denominator[:, :, None]
        mixed_low = attended.reshape(frame_rows, group_width).astype(half_kind)
        partial_out = lax.dot_general(
            mixed_low, full_output, contract_last, preferred_element_type=float_kind
        )
        middle = (
            clip_frames
            + lax.psum(partial_out.astype(jnp.bfloat16), "tp").astype(jnp.float32)
            + output_shift
        )
        normed_two, second_back = jax.vjp(layer_norm, middle, gain_two, bias_two)
        normed_two_low = normed_two.astype(half_kind)
        inner_linear = (
            jnp.dot(normed_two_low, full_inner, preferred_element_type=float_kind) + inner_shift
        )
        activated, gelu_back = jax.vjp(
            lambda value_in: jax.nn.gelu(value_in, approximate=False), inner_linear
        )
        activated_low = activated.astype(half_kind)
        partial_ffn = lax.dot_general(
            activated_low, full_outer, contract_last, preferred_element_type=float_kind
        )
        final = (
            middle
            + lax.psum(partial_ffn.astype(jnp.bfloat16), "tp").astype(jnp.float32)
            + outer_shift
        )
        results.append(final.astype(half_kind))
        back_weights = (
            lax.all_gather(shards[0], "shard", axis=0, tiled=True),
            lax.all_gather(shards[1], "shard", axis=0, tiled=True),
            lax.all_gather(shards[2], "shard", axis=0, tiled=True),
            lax.all_gather(shards[3], "shard", axis=0, tiled=True),
            lax.all_gather(shards[4], "shard", axis=0, tiled=True),
            lax.all_gather(shards[5], "shard", axis=0, tiled=True),
        )
        back_query, back_key, back_value, back_output, back_inner, back_outer = back_weights
        grad_final = cotangent[batch_index, 0].astype(float_kind) * frame_valid[:, None].astype(
            float_kind
        )
        final_low = grad_final.astype(half_kind)
        grad_outer = lax.dot_general(
            final_low, activated_low, contract_rows, preferred_element_type=float_kind
        )
        grad_activated = jnp.dot(final_low, back_outer, preferred_element_type=float_kind)
        grad_inner = gelu_back(grad_activated)[0]
        inner_low = grad_inner.astype(half_kind)
        grad_inner_weight = lax.dot_general(
            normed_two_low, inner_low, contract_rows, preferred_element_type=float_kind
        )
        partial_two = lax.dot_general(
            inner_low, back_inner, contract_last, preferred_element_type=float_kind
        )
        grad_normed_two = lax.psum(partial_two.astype(jnp.bfloat16), "tp").astype(jnp.float32)
        grad_middle_norm, grad_gain_two, grad_bias_two = second_back(grad_normed_two)
        grad_middle = grad_final + grad_middle_norm
        middle_low = grad_middle.astype(half_kind)
        grad_output_weight = lax.dot_general(
            middle_low, mixed_low, contract_rows, preferred_element_type=float_kind
        )
        grad_attended = jnp.dot(middle_low, back_output, preferred_element_type=float_kind)
        grad_heads = grad_attended.reshape(frame_rows, head_count, HD)
        scaled_grad = (grad_heads / denominator[:, :, None]).astype(half_kind)
        delta_rows = (jnp.sum(grad_heads * attended, -1) / denominator).T
        all_keys, all_values = (
            lax.all_gather(key_rows, "ctx", axis=0, tiled=True),
            lax.all_gather(value_rows, "ctx", axis=0, tiled=True),
        )

        def key_step(grad_query, block_index):
            begin = block_index * key_block
            key_part = lax.dynamic_slice_in_dim(all_keys, begin, key_block, 0).reshape(
                key_block, head_count, HD
            )
            value_part = lax.dynamic_slice_in_dim(all_values, begin, key_block, 0).reshape(
                key_block, head_count, HD
            )
            scores = (
                jnp.einsum("qhd,khd->hqk", query_heads, key_part, preferred_element_type=float_kind)
                * scaling
            )
            key_valid = begin + jnp.arange(key_block, dtype=jnp.int32) < length
            expo = jnp.where(key_valid[None, None, :], jnp.exp(scores), 0.0)
            through_values = jnp.einsum(
                "qhd,khd->hqk", scaled_grad, value_part, preferred_element_type=float_kind
            )
            grad_scores = (scaling * expo * (through_values - delta_rows[:, :, None])).astype(
                half_kind
            )
            grad_query = grad_query + jnp.einsum(
                "hqk,khd->qhd", grad_scores, key_part, preferred_element_type=float_kind
            )
            key_term = jnp.einsum(
                "hqk,qhd->khd", grad_scores, query_heads, preferred_element_type=float_kind
            )
            value_term = jnp.einsum(
                "hqk,qhd->khd",
                expo.astype(half_kind),
                scaled_grad,
                preferred_element_type=float_kind,
            )
            return (grad_query, (key_term, value_term))

        grad_query, (key_terms, value_terms) = lax.scan(
            key_step,
            jnp.zeros((frame_rows, head_count, HD), float_kind),
            jnp.arange(slot_frames // key_block),
        )
        key_terms = key_terms.reshape(slot_frames, group_width)
        value_terms = value_terms.reshape(slot_frames, group_width)
        grad_keys, grad_values = (
            lax.psum_scatter(
                key_terms.astype(jnp.bfloat16), "ctx", scatter_dimension=0, tiled=True
            ).astype(jnp.float32),
            lax.psum_scatter(
                value_terms.astype(jnp.bfloat16), "ctx", scatter_dimension=0, tiled=True
            ).astype(jnp.float32),
        )
        query_low = grad_query.reshape(frame_rows, group_width).astype(half_kind)
        keys_low = grad_keys.astype(half_kind)
        values_low = grad_values.astype(half_kind)
        grad_query_weight = lax.dot_general(
            normed_low, query_low, contract_rows, preferred_element_type=float_kind
        )
        grad_key_weight = lax.dot_general(
            normed_low, keys_low, contract_rows, preferred_element_type=float_kind
        )
        grad_value_weight = lax.dot_general(
            normed_low, values_low, contract_rows, preferred_element_type=float_kind
        )
        partial_one = lax.dot_general(
            query_low, back_query, contract_last, preferred_element_type=float_kind
        )
        partial_one = partial_one + lax.dot_general(
            keys_low, back_key, contract_last, preferred_element_type=float_kind
        )
        partial_one = partial_one + lax.dot_general(
            values_low, back_value, contract_last, preferred_element_type=float_kind
        )
        grad_normed = lax.psum(partial_one.astype(jnp.bfloat16), "tp").astype(jnp.float32)
        grad_frames_norm, grad_gain_one, grad_bias_one = first_back(grad_normed)
        frame_grads.append((grad_middle + grad_frames_norm).astype(half_kind))
        small_terms = (
            grad_gain_one,
            grad_bias_one,
            jnp.sum(query_low.astype(float_kind), 0),
            jnp.sum(values_low.astype(float_kind), 0),
            jnp.sum(grad_middle, 0),
            grad_gain_two,
            grad_bias_two,
            jnp.sum(grad_inner, 0),
            jnp.sum(grad_final, 0),
        )
        small_totals = (
            small_terms
            if small_totals is None
            else jax.tree.map(jnp.add, small_totals, small_terms)
        )
        local_grads = (
            grad_query_weight,
            grad_key_weight,
            grad_value_weight,
            grad_output_weight,
            grad_inner_weight,
            grad_outer,
        )
        scattered = (
            lax.psum_scatter(
                local_grads[0].astype(jnp.bfloat16), "shard", scatter_dimension=0, tiled=True
            ).astype(jnp.float32),
            lax.psum_scatter(
                local_grads[1].astype(jnp.bfloat16), "shard", scatter_dimension=0, tiled=True
            ).astype(jnp.float32),
            lax.psum_scatter(
                local_grads[2].astype(jnp.bfloat16), "shard", scatter_dimension=0, tiled=True
            ).astype(jnp.float32),
            lax.psum_scatter(
                local_grads[3].astype(jnp.bfloat16), "shard", scatter_dimension=0, tiled=True
            ).astype(jnp.float32),
            lax.psum_scatter(
                local_grads[4].astype(jnp.bfloat16), "shard", scatter_dimension=0, tiled=True
            ).astype(jnp.float32),
            lax.psum_scatter(
                local_grads[5].astype(jnp.bfloat16), "shard", scatter_dimension=0, tiled=True
            ).astype(jnp.float32),
        )
        contribution = (
            lax.psum(scattered[0].astype(jnp.bfloat16), "ctx").astype(jnp.float32),
            lax.psum(scattered[1].astype(jnp.bfloat16), "ctx").astype(jnp.float32),
            lax.psum(scattered[2].astype(jnp.bfloat16), "ctx").astype(jnp.float32),
            lax.psum(scattered[3].astype(jnp.bfloat16), "ctx").astype(jnp.float32),
            lax.psum(scattered[4].astype(jnp.bfloat16), "ctx").astype(jnp.float32),
            lax.psum(scattered[5].astype(jnp.bfloat16), "ctx").astype(jnp.float32),
        )
        weight_totals = (
            contribution
            if weight_totals is None
            else jax.tree.map(jnp.add, weight_totals, contribution)
        )
    small_totals = lax.psum(small_totals, ("shard", "ctx"))
    return (
        jnp.stack(results)[:, None],
        jnp.stack(frame_grads)[:, None],
        small_totals[0],
        small_totals[1],
        weight_totals[0],
        small_totals[2],
        weight_totals[1],
        weight_totals[2],
        small_totals[3],
        weight_totals[3],
        small_totals[4],
        small_totals[5],
        small_totals[6],
        weight_totals[4],
        small_totals[7],
        weight_totals[5],
        small_totals[8],
    )


def solution(mesh):
    return jax.shard_map(
        per_device,
        mesh=mesh,
        in_specs=(
            P(None, "shard", "ctx", None),
            P(None, "shard"),
            P(),
            P(),
            P("shard", "tp"),
            P("tp"),
            P("shard", "tp"),
            P("shard", "tp"),
            P("tp"),
            P("shard", "tp"),
            P(),
            P(),
            P(),
            P("shard", "tp"),
            P("tp"),
            P("shard", "tp"),
            P(),
            P(None, "shard", "ctx", None),
        ),
        out_specs=(
            P(None, "shard", "ctx", None),
            P(None, "shard", "ctx", None),
            P(),
            P(),
            P("shard", "tp"),
            P("tp"),
            P("shard", "tp"),
            P("shard", "tp"),
            P("tp"),
            P("shard", "tp"),
            P(),
            P(),
            P(),
            P("shard", "tp"),
            P("tp"),
            P("shard", "tp"),
            P(),
        ),
        check_vma=False,
    )
```

profile of v0, /device:TPU:0, one launch (start us, length us, event | category | flops | bytes accessed | tf_op | source)
XLA Modules:
  0.0 1457.8 jit_solution(4725034005878868603)
XLA Ops:
  11.6 13.1 all_gather.23
  28.1 11.4 all_gather.20
  45.2 10.5 all_gather.22
  55.8 9.7 all_gather.25
  70.5 3.0 fusion.36
  73.5 3.0 fusion.38
  76.5 3.0 fusion.32
  82.5 13.6 all-gather.7.cloned.1.call-done
  97.5 3.1 fusion.122
  109.2 37.8 %all-reduce.10.cloned.1.call-done = bf16[512,1280]{1,0:T(8,128)(2,1)} async-done(((bf16[512,1280]{1,0:T(8,128)(2,1)}), bf16[512,1280]{1,0:T(8,128)(2,1)}) %all-reduce.10.cloned.1.call-update) | async-done | bytes 1310736 | tf_op jit(solution)/shard_map/psum | solution.py:121
  160.3 24.6 %all-gather.17.cloned.1.call-done = bf16[2048,320]{0,1:T(8,128)(2,1)} async-done(((bf16[512,320]{0,1:T(8,128)(2,1)}), bf16[2048,320]{0,1:T(8,128)(2,1)}) %all-gather.17.cloned.1.call-update) | async-done | bytes 1310736 | tf_op jit(solution)/shard_map/all_gather | solution.py:90
  187.1 3.1 fusion.42
  190.2 28.3 %all-gather.15.cloned.1.call-done = bf16[2048,320]{0,1:T(8,128)(2,1)} async-done(((bf16[512,320]{0,1:T(8,128)(2,1)}), bf16[2048,320]{0,1:T(8,128)(2,1)}) %all-gather.15.cloned.1.call-update) | async-done | bytes 1310736 | tf_op jit(solution)/shard_map/all_gather | solution.py:91
  219.9 3.0 fusion.116
  235.4 35.5 %all-reduce.12.cloned.1.call-done = bf16[512,1280]{1,0:T(8,128)(2,1)} async-done(((bf16[512,1280]{1,0:T(8,128)(2,1)}), bf16[512,1280]{1,0:T(8,128)(2,1)}) %all-reduce.12.cloned.1.call-update) | async-done | bytes 1310736 | tf_op jit(solution)/shard_map/psum | solution.py:121
  273.8 6.2 all-gather.11.cloned.1.call-done
  280.0 11.7 multiply_convert_fusion.3
  292.4 8.9 multiply_convert_fusion.2
  301.3 26.4 %all-gather.13.cloned.1.call-done = bf16[1280,1280]{1,0:T(8,128)(2,1)} async-done(((bf16[640,1280]{1,0:T(8,128)(2,1)}), bf16[1280,1280]{1,0:T(8,128)(2,1)}) %all-gather.13.cloned.1.call-update) | async-done | bytes 3276816 | tf_op jit(solution)/shard_map/all_gather | solution.py:70
  327.7 7.1 fusion.280
  340.0 3.1 fusion.279
  347.2 60.0 %all-reduce.16.cloned.1.call-done = (bf16[512,1280]{1,0:T(8,128)(2,1)}, bf16[512,1280]{1,0:T(8,128)(2,1)}) async-done(((bf16[512,1280]{1,0:T(8,128)(2,1)}, bf16[512,1280]{1,0:T(8,128)(2,1)}), (bf16[512,1280]{1,0:T(8,128)(2,1)}, bf16[512,1280]{1,0:T(8,128)(2,1)})) %all-reduce.16.cloned.1.call-update) | async-done | bytes 2621456 | tf_op jit(solution)/shard_map/psum | solution.py:167
  407.2 5.5 fusion.75
  412.8 4.0 fusion.92
  423.3 60.1 %while.31 = (s32[]{:T(128)}, f32[512,4,80]{0,2,1:T(8,128)}, bf16[4,512,4,80]{1,3,2,0:T(8,128)(2,1)}, bf16[4,512,4,80]{1,3,2,0:T(8,128)(2,1)}, s32[4]{0:T(128)S(1...) while((s32[]{:T(128)}, f32[512,4,80]{0,2,1:T(8,128)}, ...), condition=%wide.region_36.37_spmd.clone, body=%wide.region_35.36_spmd.clone.sunk | while | flops 848626688 | bytes 52898636 | solution.py:217
  434.4 3.8 fusion.440
  446.4 3.1 fusion.438
  449.5 3.8 fusion.440
  461.5 3.1 fusion.438
  464.5 3.8 fusion.440
  476.5 3.1 fusion.438
  479.6 3.8 fusion.440
  498.5 60.2 %while.30 = (s32[]{:T(128)}, f32[512,4,80]{0,2,1:T(8,128)}, bf16[4,512,4,80]{1,3,2,0:T(8,128)(2,1)}, bf16[4,512,4,80]{1,3,2,0:T(8,128)(2,1)}, s32[4]{0:T(128)S(1...) while((s32[]{:T(128)}, f32[512,4,80]{0,2,1:T(8,128)}, ...), condition=%wide.region_25.26_spmd.clone, body=%wide.region_24.25_spmd.clone.sunk | while | flops 848626688 | bytes 52898636 | solution.py:217
  509.6 3.8 fusion.426
  521.6 3.1 fusion.424
  524.7 4.0 fusion.426
  536.8 3.1 fusion.424
  539.9 3.8 fusion.426
  551.9 3.1 fusion.424
  554.9 3.8 fusion.426
  570.3 3.4 convolution_convert_fusion.11
  597.3 29.0 %reduce-scatter.35.cloned.1.call-done = bf16[512,320]{0,1:T(8,128)(2,1)} async-done(((bf16[2048,320]{0,1:T(8,128)(2,1)}), bf16[512,320]{0,1:T(8,128)(2,1)}) %reduce-scatter.35.cloned.1.call-update) | async-done | bytes 327696 | tf_op jit(solution)/shard_map/reduce_scatter | solution.py:228
  629.7 5.5 convolution_convert_fusion.3
  635.3 5.5 convolution_convert_fusion.2
  640.8 5.5 convolution_convert_fusion.1
  646.4 5.4 convolution_convert_fusion
  652.4 5.4 convolution_convert_fusion.8
  673.4 17.1 %reduce-scatter.51.cloned.1.call-done = bf16[640,320]{1,0:T(8,128)(2,1)} async-done(((bf16[1280,320]{1,0:T(8,128)(2,1)}), bf16[640,320]{1,0:T(8,128)(2,1)}) %reduce-scatter.51.cloned.1.call-update) | async-done | bytes 409616
  692.5 19.9 %reduce-scatter.49.cloned.1.call-done = bf16[640,320]{1,0:T(8,128)(2,1)} async-done(((bf16[1280,320]{1,0:T(8,128)(2,1)}), bf16[640,320]{1,0:T(8,128)(2,1)}) %reduce-scatter.49.cloned.1.call-update) | async-done | bytes 409616
  714.3 19.9 %reduce-scatter.55.cloned.1.call-done = bf16[640,320]{1,0:T(8,128)(2,1)} async-done(((bf16[1280,320]{1,0:T(8,128)(2,1)}), bf16[640,320]{1,0:T(8,128)(2,1)}) %reduce-scatter.55.cloned.1.call-update) | async-done | bytes 409616
  736.2 19.9 %reduce-scatter.59.cloned.1.call-done = bf16[640,320]{1,0:T(8,128)(2,1)} async-done(((bf16[1280,320]{1,0:T(8,128)(2,1)}), bf16[640,320]{1,0:T(8,128)(2,1)}) %reduce-scatter.59.cloned.1.call-update) | async-done | bytes 409616
  758.0 19.9 %reduce-scatter.53.cloned.1.call-done = bf16[640,320]{1,0:T(8,128)(2,1)} async-done(((bf16[1280,320]{1,0:T(8,128)(2,1)}), bf16[640,320]{1,0:T(8,128)(2,1)}) %reduce-scatter.53.cloned.1.call-update) | async-done | bytes 409616
  779.8 20.0 %reduce-scatter.57.cloned.1.call-done = bf16[640,320]{1,0:T(8,128)(2,1)} async-done(((bf16[1280,320]{1,0:T(8,128)(2,1)}), bf16[640,320]{1,0:T(8,128)(2,1)}) %reduce-scatter.57.cloned.1.call-update) | async-done | bytes 409616
  801.8 45.6 %reduce-scatter.41.cloned.1.call-done = bf16[640,1280]{1,0:T(8,128)(2,1)} async-done(((bf16[1280,1280]{1,0:T(8,128)(2,1)}), bf16[640,1280]{1,0:T(8,128)(2,1)}) %reduce-scatter.41.cloned.1.call-update) | async-done | bytes 1638416 | tf_op jit(solution)/shard_map/reduce_scatter | solution.py:293
  847.4 47.7 %reduce-scatter.43.cloned.1.call-done = bf16[640,1280]{1,0:T(8,128)(2,1)} async-done(((bf16[1280,1280]{1,0:T(8,128)(2,1)}), bf16[640,1280]{1,0:T(8,128)(2,1)}) %reduce-scatter.43.cloned.1.call-update) | async-done | bytes 1638416 | tf_op jit(solution)/shard_map/reduce_scatter | solution.py:293
  895.1 47.2 %reduce-scatter.45.cloned.1.call-done = bf16[640,1280]{1,0:T(8,128)(2,1)} async-done(((bf16[1280,1280]{1,0:T(8,128)(2,1)}), bf16[640,1280]{1,0:T(8,128)(2,1)}) %reduce-scatter.45.cloned.1.call-update) | async-done | bytes 1638416 | tf_op jit(solution)/shard_map/reduce_scatter | solution.py:296
  942.3 47.2 %reduce-scatter.47.cloned.1.call-done = bf16[640,1280]{1,0:T(8,128)(2,1)} async-done(((bf16[1280,1280]{1,0:T(8,128)(2,1)}), bf16[640,1280]{1,0:T(8,128)(2,1)}) %reduce-scatter.47.cloned.1.call-update) | async-done | bytes 1638416 | tf_op jit(solution)/shard_map/reduce_scatter | solution.py:296
  990.7 103.8 %all-reduce.14.cloned.1.call-done = (bf16[512,1280]{1,0:T(8,128)(2,1)}, bf16[512,1280]{1,0:T(8,128)(2,1)}, bf16[512,1280]{1,0:T(8,128)(2,1)}, bf16[512,1280]{1,0:T(8,128)(2,1)}) async-done(((bf16[512,1280]{1,0:T(8,128)(2,1)}, bf16[512,1280]{1,0:T(8,128)(2,1)}, bf16[512,1280]{1,0:T(8,128)(2,1)}, bf16[512,1280]{1,0:T(8,128)(2,1)}), (bf16[512,1280]{1,0:T(8,128)(2,1)}, bf16[512,1280]{1,0:T(8,128)(2,1)}, ...) | async-done | bytes 5242896 | tf_op jit(solution)/shard_map/psum | solution.py:138
  1094.5 3.5 fusion.80
  1098.1 6.3 fusion.93
  1104.4 41.7 %all-reduce = (f32[1280]{0:T(1024)}, f32[1280]{0:T(1024)}, f32[320]{0:T(512)}, f32[320]{0:T(512)}, f32[1280]{0:T(1024)}, /*index=5*/f32[1280]{0:T(1024)}, f32[1280]{0:T(1024)}, f32[1280]{0:T(1024)}, f32[1280]{0:T(1024)}) all-reduce(f32[1280]{0:T(1024)S(1)} %add.526, ...), channel_id=1, replica_groups=mesh['shard'=2,'ctx'=4,'tp'=4] {'shard','ctx'}, use_global_device_ids=true, to_apply=%region_44.45 | all-reduce | flops 9600 | bytes 76800 | tf_op jit(solution)/shard_map/psum | solution.py:313
  1146.2 4.4 fusion.160
  1154.9 285.4 %all-reduce.18.cloned.1.call-done = (bf16[640,320]{0,1:T(8,128)(2,1)}, bf16[640,320]{0,1:T(8,128)(2,1)}, bf16[640,320]{0,1:T(8,128)(2,1)}, bf16[640,320]{0,1:T(8...) async-done(((bf16[640,320]{0,1:T(8,128)(2,1)}, ...) | async-done | bytes 9830416 | tf_op jit(solution)/shard_map/psum | solution.py:301
  1440.3 4.1 convert_add_fusion
  (534 shorter events, 235.8 us)
Async XLA Ops:
  8.1 3.6 copy-start.53
  8.1 60.9 %all-gather.9.cloned.1.call-start = ((), (), s32[]{:S(2)}) async-start(), calls=%async_computation.17 | async-start | bytes 1638400 | tf_op jit(solution)/shard_map/all_gather | solution.py:90
  10.6 14.7 %copy-start.77 = (f32[512]{0:T(512)}, f32[512]{0:T(512)S(1)}, u32[]{:S(2)}) copy-start(f32[512]{0:T(512)S(1)} %broadcast_multiply_fusion.3) | copy-start | bytes 6148
  11.1 14.2 copy-start.85
  11.1 138.1 %copy-start.73 = (f32[1280]{0:T(1024)}, f32[1280]{0:T(1024)S(1)}, u32[]{:S(2)}) copy-start(f32[1280]{0:T(1024)S(1)} %convert_element_type.409) | copy-start | bytes 15364
  11.6 137.6 %copy-start.75 = (f32[1280]{0:T(1024)}, f32[1280]{0:T(1024)S(1)}, u32[]{:S(2)}) copy-start(f32[1280]{0:T(1024)S(1)} %convert_element_type.410) | copy-start | bytes 15364
  28.0 15.2 %copy-start.104 = (s32[2,1]{0,1:T(1,128)S(1)}, s32[2,1]{0,1:T(1,128)}, u32[]{:S(2)}) copy-start(s32[2,1]{0,1:T(1,128)} %param.23) | copy-start | bytes 28
  28.0 17.2 %copy-start.55 = (bf16[640,320]{0,1:T(8,128)(2,1)S(1)}, bf16[640,320]{0,1:T(8,128)(2,1)}, u32[]{:S(2)}) copy-start(bf16[640,320]{0,1:T(8,128)(2,1)} %param.26) | copy-start | bytes 1228804
  28.1 68.0 %all-gather.7.cloned.1.call-start = ((), (), s32[]{:S(2)}) async-start(), calls=%async_computation.16 | async-start | bytes 1638400 | tf_op jit(solution)/shard_map/all_gather | solution.py:91
  40.5 15.3 %copy-start.56 = (bf16[640,320]{0,1:T(8,128)(2,1)S(1)}, bf16[640,320]{0,1:T(8,128)(2,1)}, u32[]{:S(2)}) copy-start(bf16[640,320]{0,1:T(8,128)(2,1)} %param.31) | copy-start | bytes 1228804
  40.5 25.6 %copy-start.106 = (bf16[320]{0:T(512)(128)(2,1)S(1)}, bf16[320]{0:T(512)(128)(2,1)}, u32[]{:S(2)}) copy-start(bf16[320]{0:T(512)(128)(2,1)} %param.27) | copy-start | bytes 1924
  43.2 103.8 %all-reduce.10.cloned.1.call-start = ((), (), s32[]{:S(2)}) async-start(), calls=%async_computation.18 | async-start | bytes 2621440 | tf_op jit(solution)/shard_map/psum | solution.py:121
  68.9 10.6 copy-start.13
  108.6 76.3 %all-gather.17.cloned.1.call-start = ((), (), s32[]{:S(2)}) async-start(), calls=%async_computation.22 | async-start | bytes 1638400 | tf_op jit(solution)/shard_map/all_gather | solution.py:90
  109.2 40.6 %copy-start.79 = (f32[512]{0:T(512)}, f32[512]{0:T(512)S(1)}, u32[]{:S(2)}) copy-start(f32[512]{0:T(512)S(1)} %broadcast_multiply_fusion.1) | copy-start | bytes 6148
  109.2 41.7 %copy-start.25 = (bf16[1280,320]{0,1:T(8,128)(2,1)S(1)}, bf16[1280,320]{0,1:T(8,128)(2,1)}, u32[]{:S(2)}) copy-start(bf16[1280,320]{0,1:T(8,128)(2,1)} %copy-done.24) | copy-start | bytes 2457604
  152.2 66.3 %all-gather.15.cloned.1.call-start = ((), (), s32[]{:S(2)}) async-start(), calls=%async_computation.21 | async-start | bytes 1638400 | tf_op jit(solution)/shard_map/all_gather | solution.py:91
  155.2 115.7 %all-reduce.12.cloned.1.call-start = ((), (), s32[]{:S(2)}) async-start(), calls=%async_computation.23 | async-start | bytes 2621440 | tf_op jit(solution)/shard_map/psum | solution.py:121
  232.6 47.4 %all-gather.11.cloned.1.call-start = ((), (), s32[]{:S(2)}) async-start(), calls=%async_computation.19 | async-start | bytes 4915200 | tf_op jit(solution)/shard_map/all_gather | solution.py:69
  233.1 94.5 %all-gather.13.cloned.1.call-start = ((), (), s32[]{:S(2)}) async-start(), calls=%async_computation.20 | async-start | bytes 4915200 | tf_op jit(solution)/shard_map/all_gather | solution.py:70
  233.7 173.5 %all-reduce.16.cloned.1.call-start = ((), (), s32[]{:S(2)}) async-start(), calls=%async_computation.41 | async-start | bytes 5242880 | tf_op jit(solution)/shard_map/psum | solution.py:167
  235.4 57.0 %copy-start.95 = (f32[1280]{0:T(1024)}, f32[1280]{0:T(1024)S(1)}, u32[]{:S(2)}) copy-start(f32[1280]{0:T(1024)S(1)} %convert_element_type.427) | copy-start | bytes 15364
  280.0 11.7 copy-start.5
  280.0 12.4 copy-start.109
  327.7 7.1 copy-start.110
  334.8 3.7 copy-start.107
  334.8 4.4 copy-start.115
  334.8 5.2 copy-start.116
  347.1 237.2 %reduce-scatter.37.cloned.1.call-start = ((), (), s32[]{:S(2)}) async-start(), calls=%async_computation.26 | async-start | bytes 1638400 | tf_op jit(solution)/shard_map/reduce_scatter | solution.py:225
  407.2 5.5 copy-start.6
  407.2 5.6 copy-start.8
  407.2 5.6 copy-start.21
  407.2 5.6 copy-start.22
  412.8 4.0 copy-start.35
  487.2 100.7 %reduce-scatter.39.cloned.1.call-start = ((), (), s32[]{:S(2)}) async-start(), calls=%async_computation.27 | async-start | bytes 1638400 | tf_op jit(solution)/shard_map/reduce_scatter | solution.py:228
  487.2 4.0 copy-start.9
  487.2 3.9 copy-start.23
  487.3 3.9 copy-start.36
  496.0 97.8 %reduce-scatter.33.cloned.1.call-start = ((), (), s32[]{:S(2)}) async-start(), calls=%async_computation.24 | async-start | bytes 1638400 | tf_op jit(solution)/shard_map/reduce_scatter | solution.py:225
  562.5 63.8 %reduce-scatter.35.cloned.1.call-start = ((), (), s32[]{:S(2)}) async-start(), calls=%async_computation.25 | async-start | bytes 1638400 | tf_op jit(solution)/shard_map/reduce_scatter | solution.py:228
  566.3 103.1 %reduce-scatter.63.cloned.1.call-start = ((), (), s32[]{:S(2)}) async-start(), calls=%async_computation.39 | async-start | bytes 1474560
  570.2 5.8 copy-start.15
  570.2 101.3 %reduce-scatter.61.cloned.1.call-start = ((), (), s32[]{:S(2)}) async-start(), calls=%async_computation.38 | async-start | bytes 1474560
  575.9 114.6 %reduce-scatter.51.cloned.1.call-start = ((), (), s32[]{:S(2)}) async-start(), calls=%async_computation.33 | async-start | bytes 1474560
  580.9 131.4 %reduce-scatter.49.cloned.1.call-start = ((), (), s32[]{:S(2)}) async-start(), calls=%async_computation.32 | async-start | bytes 1474560
  584.3 149.9 %reduce-scatter.55.cloned.1.call-start = ((), (), s32[]{:S(2)}) async-start(), calls=%async_computation.35 | async-start | bytes 1474560
  587.8 168.3 %reduce-scatter.59.cloned.1.call-start = ((), (), s32[]{:S(2)}) async-start(), calls=%async_computation.37 | async-start | bytes 1474560
  591.2 186.7 %reduce-scatter.53.cloned.1.call-start = ((), (), s32[]{:S(2)}) async-start(), calls=%async_computation.34 | async-start | bytes 1474560
  597.2 32.5 %copy-start.96 = (f32[1280]{0:T(1024)S(1)}, f32[1280]{0:T(1024)}, u32[]{:S(2)}) copy-start(f32[1280]{0:T(1024)} %copy-done.95) | copy-start | bytes 15364
  597.2 202.6 %reduce-scatter.57.cloned.1.call-start = ((), (), s32[]{:S(2)}) async-start(), calls=%async_computation.36 | async-start | bytes 1474560
  629.6 217.8 %reduce-scatter.41.cloned.1.call-start = ((), (), s32[]{:S(2)}) async-start(), calls=%async_computation.28 | async-start | bytes 4915200 | tf_op jit(solution)/shard_map/reduce_scatter | solution.py:293
  635.2 259.9 %reduce-scatter.43.cloned.1.call-start = ((), (), s32[]{:S(2)}) async-start(), calls=%async_computation.29 | async-start | bytes 4915200 | tf_op jit(solution)/shard_map/reduce_scatter | solution.py:293
  640.8 301.5 %reduce-scatter.45.cloned.1.call-start = ((), (), s32[]{:S(2)}) async-start(), calls=%async_computation.30 | async-start | bytes 4915200 | tf_op jit(solution)/shard_map/reduce_scatter | solution.py:296
  646.4 343.1 %reduce-scatter.47.cloned.1.call-start = ((), (), s32[]{:S(2)}) async-start(), calls=%async_computation.31 | async-start | bytes 4915200 | tf_op jit(solution)/shard_map/reduce_scatter | solution.py:296
  651.9 442.6 %all-reduce.14.cloned.1.call-start = ((), (), s32[]{:S(2)}) async-start(), calls=%async_computation.40 | async-start | bytes 10485760 | tf_op jit(solution)/shard_map/psum | solution.py:138
  652.3 5.5 copy-start.108
  652.4 5.5 copy-start.112
  669.2 771.1 %all-reduce.18.cloned.1.call-start = ((), (), s32[]{:S(2)}) async-start(), calls=%async_computation.42 | async-start | bytes 19660800 | tf_op jit(solution)/shard_map/psum | solution.py:301
  1094.5 3.6 copy-start.7
  1094.5 3.6 copy-start.10
  1094.5 3.6 copy-start.19
  1094.5 3.6 copy-start.20
  1440.3 4.1 copy-start.43
  1440.3 4.1 copy-start.44
  (104 other events, 213.8 us)
Sparse Core Ops, SparseCore 0:
  28.2 33.9 all-gather.8
  64.3 31.6 all-gather.6
  108.7 38.2 all-reduce.9
  152.4 32.5 all-gather.16
  186.9 31.6 all-gather.14
  232.7 38.2 all-reduce.11
  347.2 59.9 all-reduce.15
  487.3 31.4 reduce-scatter.36
  521.7 30.0 reduce-scatter.38
  562.6 31.2 reduce-scatter.32
  596.2 30.0 reduce-scatter.34
  628.4 18.3 reduce-scatter.62
  649.0 19.6 reduce-scatter.60
  670.8 19.6 reduce-scatter.50
  692.6 19.6 reduce-scatter.48
  714.5 19.6 reduce-scatter.54
  736.3 19.6 reduce-scatter.58
  758.1 19.6 reduce-scatter.52
  780.1 19.6 reduce-scatter.56
  802.5 44.8 reduce-scatter.40
  850.2 44.8 reduce-scatter.42
  897.4 44.8 reduce-scatter.44
  944.6 44.8 reduce-scatter.46
  991.9 102.5 all-reduce.13
  1099.9 340.3 all-reduce.17
Sparse Core Ops, SparseCore 1:
  234.6 45.3 all-gather.10
  281.4 46.2 all-gather.12
where the time goes:
time: 1470 us; the launch traced here: 1460 us
  waiting for transfers between devices  959 us (65%)
  matrix products  225 us (15%)
  local copies, waits for them, and re-layouts  97 us (7%)
  blocking collectives  86.5 us (6%)
  other arithmetic  63.9 us (4%)
  between operations  18.4 us (1%)
    psum x1, waiting for transfers between devices, per_device(): lax.psum(scattered[0].astype(jnp.bfloat16), 'ctx').astype(jnp.float32)  285 us
    unnamed x35, waiting for transfers between devices  118 us
    psum x1, waiting for transfers between devices, per_device(): lax.psum(partial_ffn.astype(jnp.bfloat16), 'tp').astype(jnp.float32)  104 us
    reduce_scatter x2, waiting for transfers between devices, per_device(): lax.psum_scatter(local_grads[5].astype(jnp.bfloat16), 'shard', scatter_di...  94.3 us
    reduce_scatter x2, waiting for transfers between devices, per_device(): lax.psum_scatter(local_grads[4].astype(jnp.bfloat16), 'shard', scatter_di...  93.3 us
    psum x2, waiting for transfers between devices, per_device(): lax.psum(partial_out.astype(jnp.bfloat16), 'tp').astype(jnp.float32)  73.4 us
    psum x1, waiting for transfers between devices, per_device(): lax.psum(partial_two.astype(jnp.bfloat16), 'tp').astype(jnp.float32)  60 us
    unnamed x238, local copies, waits for them, and re-layouts  51.3 us
  transfers between devices with their start and end apart: 27, of which 22 were waited for; matrix products, arithmetic and copies ran while one was open for 16% of the time, Pallas kernels for 0%

commit v1 on v0

--- a/solution.py
+++ b/solution.py
@@ -118,7 +118,9 @@
         )
         middle = (
             clip_frames
-            + lax.psum(partial_out.astype(jnp.bfloat16), "tp").astype(jnp.float32)
+            + jnp.sum(lax.all_gather(partial_out.astype(jnp.bfloat16), "tp"), axis=0).astype(
+                jnp.float32
+            )
             + output_shift
         )
         normed_two, second_back = jax.vjp(layer_norm, middle, gain_two, bias_two)

time: 1470 us -> 1510 us (1.027)
  waiting for transfers between devices: 959 us -> 997 us
    all_gather x0 -> x2, waiting for transfers between devices: none -> 75.8 us  [per_device(): lax.all_gather(partial_out.astype(jnp.bfloat16), 'tp')]
    psum x2 -> x0, waiting for transfers between devices: 73.4 us -> none  [per_device(): lax.psum(partial_out.astype(jnp.bfloat16), 'tp').astype(jnp.float32)]
    all_gather x1, waiting for transfers between devices: 6.2 us -> 40.4 us  [per_device(): lax.all_gather(shards[4], 'shard', axis=0, tiled=True)]
    unnamed x238 -> x240, local copies, waits for them, and re-layouts: 51.3 us -> 51.3 us
where the time goes in v1:
time: 1510 us; the launch traced here: 1500 us
  waiting for transfers between devices  997 us (66%)
  matrix products  225 us (15%)
  local copies, waits for them, and re-layouts  96.9 us (6%)
  blocking collectives  86.6 us (6%)
  other arithmetic  72.6 us (5%)
  between operations  17.2 us (1%)
    psum x1, waiting for transfers between devices, per_device(): lax.psum(scattered[0].astype(jnp.bfloat16), 'ctx').astype(jnp.float32)  285 us
    unnamed x35, waiting for transfers between devices  118 us
    psum x1, waiting for transfers between devices, per_device(): lax.psum(partial_ffn.astype(jnp.bfloat16), 'tp').astype(jnp.float32)  104 us
    reduce_scatter x2, waiting for transfers between devices, per_device(): lax.psum_scatter(local_grads[5].astype(jnp.bfloat16), 'shard', scatter_di...  94.1 us
    reduce_scatter x2, waiting for transfers between devices, per_device(): lax.psum_scatter(local_grads[4].astype(jnp.bfloat16), 'shard', scatter_di...  93.5 us
    all_gather x2, waiting for transfers between devices, per_device(): lax.all_gather(partial_out.astype(jnp.bfloat16), 'tp')  75.8 us
    psum x1, waiting for transfers between devices, per_device(): lax.psum(partial_two.astype(jnp.bfloat16), 'tp').astype(jnp.float32)  60 us
    unnamed x240, local copies, waits for them, and re-layouts  51.3 us
  transfers between devices with their start and end apart: 27, of which 22 were waited for; matrix products, arithmetic and copies ran while one was open for 16% of the time, Pallas kernels for 0%

profile of v1, /device:TPU:0, one launch (start us, length us, event | category | flops | bytes accessed | tf_op | source)
XLA Modules:
  0.0 1502.7 jit_solution(2736862184695648874)
XLA Ops:
  10.8 13.1 all_gather.31
  27.3 11.4 all_gather.28
  44.4 10.5 all_gather.30
  55.0 9.7 all_gather.33
  72.8 3.1 fusion.38
  76.0 3.1 fusion.32
  82.1 13.1 all-gather.11.cloned.1.call-done
  96.5 3.1 fusion.122
  108.3 39.2 %all-gather.23.cloned.1.call-done = bf16[2048,1280]{1,0:T(8,128)(2,1)} async-done(((bf16[512,1280]{1,0:T(8,128)(2,1)}), bf16[2048,1280]{1,0:T(8,128)(2,1)}) %all-gather.23.cloned.1.call-update) | async-done | bytes 5242896 | tf_op jit(solution)/shard_map/all_gather | solution.py:121
  147.4 4.7 reduce_sum.429
  164.7 25.5 %all-gather.21.cloned.1.call-done = bf16[2048,320]{0,1:T(8,128)(2,1)} async-done(((bf16[512,320]{0,1:T(8,128)(2,1)}), bf16[2048,320]{0,1:T(8,128)(2,1)}) %all-gather.21.cloned.1.call-update) | async-done | bytes 1310736 | tf_op jit(solution)/shard_map/all_gather | solution.py:90
  192.3 3.1 fusion.42
  195.4 28.4 %all-gather.19.cloned.1.call-done = bf16[2048,320]{0,1:T(8,128)(2,1)} async-done(((bf16[512,320]{0,1:T(8,128)(2,1)}), bf16[2048,320]{0,1:T(8,128)(2,1)}) %all-gather.19.cloned.1.call-update) | async-done | bytes 1310736 | tf_op jit(solution)/shard_map/all_gather | solution.py:91
  240.9 36.6 %all-gather.25.cloned.1.call-done = bf16[2048,1280]{1,0:T(8,128)(2,1)} async-done(((bf16[512,1280]{1,0:T(8,128)(2,1)}), bf16[2048,1280]{1,0:T(8,128)(2,1)}) %all-gather.25.cloned.1.call-update) | async-done | bytes 5242896 | tf_op jit(solution)/shard_map/all_gather | solution.py:121
  277.5 4.7 reduce_sum.503
  285.0 40.4 %all-gather.15.cloned.1.call-done = bf16[1280,1280]{1,0:T(8,128)(2,1)} async-done(((bf16[640,1280]{1,0:T(8,128)(2,1)}), bf16[1280,1280]{1,0:T(8,128)(2,1)}) %all-gather.15.cloned.1.call-update) | async-done | bytes 3276816 | tf_op jit(solution)/shard_map/all_gather | solution.py:69
  325.4 11.7 multiply_convert_fusion.3
  337.8 8.9 multiply_convert_fusion.2
  346.7 26.7 %all-gather.17.cloned.1.call-done = bf16[1280,1280]{1,0:T(8,128)(2,1)} async-done(((bf16[640,1280]{1,0:T(8,128)(2,1)}), bf16[1280,1280]{1,0:T(8,128)(2,1)}) %all-gather.17.cloned.1.call-update) | async-done | bytes 3276816 | tf_op jit(solution)/shard_map/all_gather | solution.py:70
  373.4 7.1 fusion.280
  385.7 3.1 fusion.279
  392.9 60.0 %all-reduce.10.cloned.1.call-done = (bf16[512,1280]{1,0:T(8,128)(2,1)}, bf16[512,1280]{1,0:T(8,128)(2,1)}) async-done(((bf16[512,1280]{1,0:T(8,128)(2,1)}, bf16[512,1280]{1,0:T(8,128)(2,1)}), (bf16[512,1280]{1,0:T(8,128)(2,1)}, bf16[512,1280]{1,0:T(8,128)(2,1)})) %all-reduce.10.cloned.1.call-update) | async-done | bytes 2621456 | tf_op jit(solution)/shard_map/psum | solution.py:169
  452.9 5.5 fusion.75
  458.5 4.0 fusion.92
  468.9 59.5 %while.31 = (s32[]{:T(128)}, f32[512,4,80]{0,2,1:T(8,128)}, bf16[4,512,4,80]{1,3,2,0:T(8,128)(2,1)}, bf16[4,512,4,80]{1,3,2,0:T(8,128)(2,1)}, s32[4]{0:T(128)S(1...) while((s32[]{:T(128)}, f32[512,4,80]{0,2,1:T(8,128)}, ...), condition=%wide.region_36.37_spmd.clone, body=%wide.region_35.36_spmd.clone.sunk | while | flops 848626688 | bytes 52898636 | solution.py:219
  479.9 3.8 fusion.440
  491.8 3.1 fusion.438
  494.8 3.8 fusion.440
  506.7 3.1 fusion.438
  509.7 3.8 fusion.440
  521.6 3.1 fusion.438
  524.6 3.8 fusion.440
  543.5 60.4 %while.30 = (s32[]{:T(128)}, f32[512,4,80]{0,2,1:T(8,128)}, bf16[4,512,4,80]{1,3,2,0:T(8,128)(2,1)}, bf16[4,512,4,80]{1,3,2,0:T(8,128)(2,1)}, s32[4]{0:T(128)S(1...) while((s32[]{:T(128)}, f32[512,4,80]{0,2,1:T(8,128)}, ...), condition=%wide.region_25.26_spmd.clone, body=%wide.region_24.25_spmd.clone.sunk | while | flops 848626688 | bytes 52898636 | solution.py:219
  554.7 3.8 fusion.426
  566.7 3.1 fusion.424
  569.8 4.0 fusion.426
  582.0 3.1 fusion.424
  585.0 3.8 fusion.426
  597.1 3.1 fusion.424
  600.1 3.8 fusion.426
  615.5 3.4 convolution_convert_fusion.11
  642.5 29.0 %reduce-scatter.35.cloned.1.call-done = bf16[512,320]{0,1:T(8,128)(2,1)} async-done(((bf16[2048,320]{0,1:T(8,128)(2,1)}), bf16[512,320]{0,1:T(8,128)(2,1)}) %reduce-scatter.35.cloned.1.call-update) | async-done | bytes 327696 | tf_op jit(solution)/shard_map/reduce_scatter | solution.py:230
  674.9 5.5 convolution_convert_fusion.3
  680.5 5.5 convolution_convert_fusion.2
  686.1 5.5 convolution_convert_fusion.1
  691.7 5.4 convolution_convert_fusion
  697.6 5.5 convolution_convert_fusion.8
  718.7 17.0 %reduce-scatter.51.cloned.1.call-done = bf16[640,320]{1,0:T(8,128)(2,1)} async-done(((bf16[1280,320]{1,0:T(8,128)(2,1)}), bf16[640,320]{1,0:T(8,128)(2,1)}) %reduce-scatter.51.cloned.1.call-update) | async-done | bytes 409616
  737.6 19.9 %reduce-scatter.49.cloned.1.call-done = bf16[640,320]{1,0:T(8,128)(2,1)} async-done(((bf16[1280,320]{1,0:T(8,128)(2,1)}), bf16[640,320]{1,0:T(8,128)(2,1)}) %reduce-scatter.49.cloned.1.call-update) | async-done | bytes 409616
  759.4 19.9 %reduce-scatter.55.cloned.1.call-done = bf16[640,320]{1,0:T(8,128)(2,1)} async-done(((bf16[1280,320]{1,0:T(8,128)(2,1)}), bf16[640,320]{1,0:T(8,128)(2,1)}) %reduce-scatter.55.cloned.1.call-update) | async-done | bytes 409616
  781.3 20.0 %reduce-scatter.59.cloned.1.call-done = bf16[640,320]{1,0:T(8,128)(2,1)} async-done(((bf16[1280,320]{1,0:T(8,128)(2,1)}), bf16[640,320]{1,0:T(8,128)(2,1)}) %reduce-scatter.59.cloned.1.call-update) | async-done | bytes 409616
  803.3 19.8 %reduce-scatter.53.cloned.1.call-done = bf16[640,320]{1,0:T(8,128)(2,1)} async-done(((bf16[1280,320]{1,0:T(8,128)(2,1)}), bf16[640,320]{1,0:T(8,128)(2,1)}) %reduce-scatter.53.cloned.1.call-update) | async-done | bytes 409616
  825.1 20.0 %reduce-scatter.57.cloned.1.call-done = bf16[640,320]{1,0:T(8,128)(2,1)} async-done(((bf16[1280,320]{1,0:T(8,128)(2,1)}), bf16[640,320]{1,0:T(8,128)(2,1)}) %reduce-scatter.57.cloned.1.call-update) | async-done | bytes 409616
  847.1 45.7 %reduce-scatter.41.cloned.1.call-done = bf16[640,1280]{1,0:T(8,128)(2,1)} async-done(((bf16[1280,1280]{1,0:T(8,128)(2,1)}), bf16[640,1280]{1,0:T(8,128)(2,1)}) %reduce-scatter.41.cloned.1.call-update) | async-done | bytes 1638416 | tf_op jit(solution)/shard_map/reduce_scatter | solution.py:295
  892.8 47.7 %reduce-scatter.43.cloned.1.call-done = bf16[640,1280]{1,0:T(8,128)(2,1)} async-done(((bf16[1280,1280]{1,0:T(8,128)(2,1)}), bf16[640,1280]{1,0:T(8,128)(2,1)}) %reduce-scatter.43.cloned.1.call-update) | async-done | bytes 1638416 | tf_op jit(solution)/shard_map/reduce_scatter | solution.py:295
  940.5 47.0 %reduce-scatter.45.cloned.1.call-done = bf16[640,1280]{1,0:T(8,128)(2,1)} async-done(((bf16[1280,1280]{1,0:T(8,128)(2,1)}), bf16[640,1280]{1,0:T(8,128)(2,1)}) %reduce-scatter.45.cloned.1.call-update) | async-done | bytes 1638416 | tf_op jit(solution)/shard_map/reduce_scatter | solution.py:298
  987.5 47.1 %reduce-scatter.47.cloned.1.call-done = bf16[640,1280]{1,0:T(8,128)(2,1)} async-done(((bf16[1280,1280]{1,0:T(8,128)(2,1)}), bf16[640,1280]{1,0:T(8,128)(2,1)}) %reduce-scatter.47.cloned.1.call-update) | async-done | bytes 1638416 | tf_op jit(solution)/shard_map/reduce_scatter | solution.py:298
  1035.9 103.8 %all-reduce.8.cloned.1.call-done = (bf16[512,1280]{1,0:T(8,128)(2,1)}, bf16[512,1280]{1,0:T(8,128)(2,1)}, bf16[512,1280]{1,0:T(8,128)(2,1)}, bf16[512,1280]{1,0:T(8,128)(2,1)}) async-done(((bf16[512,1280]{1,0:T(8,128)(2,1)}, bf16[512,1280]{1,0:T(8,128)(2,1)}, bf16[512,1280]{1,0:T(8,128)(2,1)}, bf16[512,1280]{1,0:T(8,128)(2,1)}), (bf16[512,1280]{1,0:T(8,128)(2,1)}, bf16[512,1280]{1,0:T(8,128)(2,1)}, ...) | async-done | bytes 5242896 | tf_op jit(solution)/shard_map/psum | solution.py:140
  1139.8 3.5 fusion.80
  1143.3 6.3 fusion.93
  1149.7 41.8 %all-reduce = (f32[1280]{0:T(1024)}, f32[1280]{0:T(1024)}, f32[320]{0:T(512)}, f32[320]{0:T(512)}, f32[1280]{0:T(1024)}, /*index=5*/f32[1280]{0:T(1024)}, f32[1280]{0:T(1024)}, f32[1280]{0:T(1024)}, f32[1280]{0:T(1024)}) all-reduce(f32[1280]{0:T(1024)S(1)} %add.522, ...), channel_id=1, replica_groups=mesh['shard'=2,'ctx'=4,'tp'=4] {'shard','ctx'}, use_global_device_ids=true, to_apply=%region_44.45 | all-reduce | flops 9600 | bytes 76800 | tf_op jit(solution)/shard_map/psum | solution.py:315
  1191.5 4.4 fusion.160
  1200.3 285.2 %all-reduce.12.cloned.1.call-done = (bf16[640,320]{0,1:T(8,128)(2,1)}, bf16[640,320]{0,1:T(8,128)(2,1)}, bf16[640,320]{0,1:T(8,128)(2,1)}, bf16[640,320]{0,1:T(8...) async-done(((bf16[640,320]{0,1:T(8,128)(2,1)}, ...) | async-done | bytes 9830416 | tf_op jit(solution)/shard_map/psum | solution.py:303
  1485.4 4.1 convert_add_fusion
  (538 shorter events, 241.1 us)
Async XLA Ops:
  7.2 3.6 copy-start.54
  7.2 61.0 %all-gather.13.cloned.1.call-start = ((), (), s32[]{:S(2)}) async-start(), calls=%async_computation.17 | async-start | bytes 1638400 | tf_op jit(solution)/shard_map/all_gather | solution.py:90
  9.7 14.7 copy-start.78
  10.2 14.2 copy-start.86
  10.3 144.1 %copy-start.74 = (f32[1280]{0:T(1024)}, f32[1280]{0:T(1024)S(1)}, u32[]{:S(2)}) copy-start(f32[1280]{0:T(1024)S(1)} %convert_element_type.413) | copy-start | bytes 15364
  10.8 143.6 %copy-start.76 = (f32[1280]{0:T(1024)}, f32[1280]{0:T(1024)S(1)}, u32[]{:S(2)}) copy-start(f32[1280]{0:T(1024)S(1)} %convert_element_type.414) | copy-start | bytes 15364
  27.2 15.2 %copy-start.105 = (s32[2,1]{0,1:T(1,128)S(1)}, s32[2,1]{0,1:T(1,128)}, u32[]{:S(2)}) copy-start(s32[2,1]{0,1:T(1,128)} %param.23) | copy-start | bytes 28
  27.2 17.2 %copy-start.56 = (bf16[640,320]{0,1:T(8,128)(2,1)S(1)}, bf16[640,320]{0,1:T(8,128)(2,1)}, u32[]{:S(2)}) copy-start(bf16[640,320]{0,1:T(8,128)(2,1)} %param.26) | copy-start | bytes 1228804
  27.2 67.9 %all-gather.11.cloned.1.call-start = ((), (), s32[]{:S(2)}) async-start(), calls=%async_computation.16 | async-start | bytes 1638400 | tf_op jit(solution)/shard_map/all_gather | solution.py:91
  39.6 15.4 %copy-start.57 = (bf16[640,320]{0,1:T(8,128)(2,1)S(1)}, bf16[640,320]{0,1:T(8,128)(2,1)}, u32[]{:S(2)}) copy-start(bf16[640,320]{0,1:T(8,128)(2,1)} %param.31) | copy-start | bytes 1228804
  39.6 25.7 %copy-start.107 = (bf16[320]{0:T(512)(128)(2,1)S(1)}, bf16[320]{0:T(512)(128)(2,1)}, u32[]{:S(2)}) copy-start(bf16[320]{0:T(512)(128)(2,1)} %param.27) | copy-start | bytes 1924
  42.4 105.1 %all-gather.23.cloned.1.call-start = ((), (), s32[]{:S(2)}) async-start(), calls=%async_computation.30 | async-start | bytes 6553600 | tf_op jit(solution)/shard_map/all_gather | solution.py:121
  68.2 10.8 copy-start.13
  107.7 82.4 %all-gather.21.cloned.1.call-start = ((), (), s32[]{:S(2)}) async-start(), calls=%async_computation.21 | async-start | bytes 1638400 | tf_op jit(solution)/shard_map/all_gather | solution.py:90
  108.3 46.2 %copy-start.80 = (f32[512]{0:T(512)}, f32[512]{0:T(512)S(1)}, u32[]{:S(2)}) copy-start(f32[512]{0:T(512)S(1)} %broadcast_multiply_fusion.1) | copy-start | bytes 6148
  152.1 3.9 copy-start.25
  157.5 66.3 %all-gather.19.cloned.1.call-start = ((), (), s32[]{:S(2)}) async-start(), calls=%async_computation.20 | async-start | bytes 1638400 | tf_op jit(solution)/shard_map/all_gather | solution.py:91
  160.2 117.2 %all-gather.25.cloned.1.call-start = ((), (), s32[]{:S(2)}) async-start(), calls=%async_computation.31 | async-start | bytes 6553600 | tf_op jit(solution)/shard_map/all_gather | solution.py:121
  237.8 87.6 %all-gather.15.cloned.1.call-start = ((), (), s32[]{:S(2)}) async-start(), calls=%async_computation.18 | async-start | bytes 4915200 | tf_op jit(solution)/shard_map/all_gather | solution.py:69
  238.5 134.8 %all-gather.17.cloned.1.call-start = ((), (), s32[]{:S(2)}) async-start(), calls=%async_computation.19 | async-start | bytes 4915200 | tf_op jit(solution)/shard_map/all_gather | solution.py:70
  239.3 213.6 %all-reduce.10.cloned.1.call-start = ((), (), s32[]{:S(2)}) async-start(), calls=%async_computation.41 | async-start | bytes 5242880 | tf_op jit(solution)/shard_map/psum | solution.py:169
  240.8 97.0 %copy-start.96 = (f32[1280]{0:T(1024)}, f32[1280]{0:T(1024)S(1)}, u32[]{:S(2)}) copy-start(f32[1280]{0:T(1024)S(1)} %convert_element_type.431) | copy-start | bytes 15364
  325.4 11.7 copy-start.5
  325.4 12.4 copy-start.110
  373.4 7.1 copy-start.111
  380.5 3.7 copy-start.108
  380.5 4.4 copy-start.116
  380.5 5.2 copy-start.117
  392.8 236.7 %reduce-scatter.37.cloned.1.call-start = ((), (), s32[]{:S(2)}) async-start(), calls=%async_computation.24 | async-start | bytes 1638400 | tf_op jit(solution)/shard_map/reduce_scatter | solution.py:227
  452.9 5.5 copy-start.6
  452.9 5.5 copy-start.8
  452.9 5.5 copy-start.21
  452.9 5.5 copy-start.22
  458.5 4.0 copy-start.36
  532.2 100.8 %reduce-scatter.39.cloned.1.call-start = ((), (), s32[]{:S(2)}) async-start(), calls=%async_computation.25 | async-start | bytes 1638400 | tf_op jit(solution)/shard_map/reduce_scatter | solution.py:230
  532.3 4.0 copy-start.9
  532.3 3.9 copy-start.23
  532.3 3.9 copy-start.37
  541.0 98.1 %reduce-scatter.33.cloned.1.call-start = ((), (), s32[]{:S(2)}) async-start(), calls=%async_computation.22 | async-start | bytes 1638400 | tf_op jit(solution)/shard_map/reduce_scatter | solution.py:227
  607.7 63.8 %reduce-scatter.35.cloned.1.call-start = ((), (), s32[]{:S(2)}) async-start(), calls=%async_computation.23 | async-start | bytes 1638400 | tf_op jit(solution)/shard_map/reduce_scatter | solution.py:230
  611.6 103.1 %reduce-scatter.63.cloned.1.call-start = ((), (), s32[]{:S(2)}) async-start(), calls=%async_computation.39 | async-start | bytes 1474560
  615.4 5.8 copy-start.15
  615.4 101.3 %reduce-scatter.61.cloned.1.call-start = ((), (), s32[]{:S(2)}) async-start(), calls=%async_computation.38 | async-start | bytes 1474560
  621.2 114.5 %reduce-scatter.51.cloned.1.call-start = ((), (), s32[]{:S(2)}) async-start(), calls=%async_computation.33 | async-start | bytes 1474560
  626.2 131.3 %reduce-scatter.49.cloned.1.call-start = ((), (), s32[]{:S(2)}) async-start(), calls=%async_computation.32 | async-start | bytes 1474560
  629.5 149.8 %reduce-scatter.55.cloned.1.call-start = ((), (), s32[]{:S(2)}) async-start(), calls=%async_computation.35 | async-start | bytes 1474560
  633.0 168.3 %reduce-scatter.59.cloned.1.call-start = ((), (), s32[]{:S(2)}) async-start(), calls=%async_computation.37 | async-start | bytes 1474560
  636.4 186.7 %reduce-scatter.53.cloned.1.call-start = ((), (), s32[]{:S(2)}) async-start(), calls=%async_computation.34 | async-start | bytes 1474560
  642.5 32.4 %copy-start.97 = (f32[1280]{0:T(1024)S(1)}, f32[1280]{0:T(1024)}, u32[]{:S(2)}) copy-start(f32[1280]{0:T(1024)} %copy-done.96) | copy-start | bytes 15364
  642.5 202.6 %reduce-scatter.57.cloned.1.call-start = ((), (), s32[]{:S(2)}) async-start(), calls=%async_computation.36 | async-start | bytes 1474560
  674.9 218.0 %reduce-scatter.41.cloned.1.call-start = ((), (), s32[]{:S(2)}) async-start(), calls=%async_computation.26 | async-start | bytes 4915200 | tf_op jit(solution)/shard_map/reduce_scatter | solution.py:295
  680.4 260.1 %reduce-scatter.43.cloned.1.call-start = ((), (), s32[]{:S(2)}) async-start(), calls=%async_computation.27 | async-start | bytes 4915200 | tf_op jit(solution)/shard_map/reduce_scatter | solution.py:295
  686.0 301.5 %reduce-scatter.45.cloned.1.call-start = ((), (), s32[]{:S(2)}) async-start(), calls=%async_computation.28 | async-start | bytes 4915200 | tf_op jit(solution)/shard_map/reduce_scatter | solution.py:298
  691.6 343.1 %reduce-scatter.47.cloned.1.call-start = ((), (), s32[]{:S(2)}) async-start(), calls=%async_computation.29 | async-start | bytes 4915200 | tf_op jit(solution)/shard_map/reduce_scatter | solution.py:298
  697.1 442.6 %all-reduce.8.cloned.1.call-start = ((), (), s32[]{:S(2)}) async-start(), calls=%async_computation.40 | async-start | bytes 10485760 | tf_op jit(solution)/shard_map/psum | solution.py:140
  697.6 5.5 copy-start.109
  697.6 5.5 copy-start.113
  714.5 771.0 %all-reduce.12.cloned.1.call-start = ((), (), s32[]{:S(2)}) async-start(), calls=%async_computation.42 | async-start | bytes 19660800 | tf_op jit(solution)/shard_map/psum | solution.py:303
  1139.7 3.6 copy-start.7
  1139.8 3.6 copy-start.10
  1139.8 3.6 copy-start.19
  1139.8 3.6 copy-start.20
  1485.4 4.1 copy-start.44
  1485.4 4.1 copy-start.45
  (105 other events, 216.6 us)
Sparse Core Ops, SparseCore 0:
  27.3 33.9 all-gather.12
  63.5 31.5 all-gather.10
  107.8 39.5 all-gather.22
  157.6 32.5 all-gather.20
  192.1 31.6 all-gather.18
  237.9 39.5 all-gather.24
  279.0 46.3 all-gather.14
  327.0 46.3 all-gather.16
  392.9 59.9 all-reduce.9
  532.3 31.4 reduce-scatter.36
  566.7 30.0 reduce-scatter.38
  607.8 31.2 reduce-scatter.32
  641.4 30.0 reduce-scatter.34
  673.6 18.3 reduce-scatter.62
  694.1 19.6 reduce-scatter.60
  715.9 19.6 reduce-scatter.50
  737.8 19.6 reduce-scatter.48
  759.6 19.6 reduce-scatter.54
  781.6 19.6 reduce-scatter.58
  803.4 19.6 reduce-scatter.52
  825.4 19.6 reduce-scatter.56
  847.9 44.8 reduce-scatter.40
  895.6 44.8 reduce-scatter.42
  942.6 44.8 reduce-scatter.44
  989.8 44.8 reduce-scatter.46
  1037.1 102.5 all-reduce.7
  1145.0 340.4 all-reduce.11
